TPU v7x, 512 devices: a whole 4x4x16 slice. The times are simulated.
512 devices in a mesh: region: 64 (over z, x), split: 8 (over y, core).
Axes of the slice: x: 4, y: 4, z: 16, core: 2. Of those that a mesh axis runs over, the one named last changes fastest.
Arguments:
- vectors: float32 [294912, 256], P(('region', 'split'))
- hessian: bfloat16 [1536, 12, 192, 192], P(('region', 'split')), may hold values from -0.125 to 0.125
- block_cols: int32 [1536, 12], P(('region', 'split')), may hold values from 0 to 35, as said below
- live_blocks: int32 [1536], P(('region', 'split')), may hold values from 6 to 12, as said below
- halo_lists: int32 [64, 2, 6], P('region'), may hold values from 0 to 23, as said below
- bounds: float32 [2], replicated, as said below
Outputs:
- basis: float32 [294912, 256], P(('region', 'split'))
- projected: float32 [256, 256], replicated
Inputs may be any that keep to these rules, and one draw needn't show every extreme that they name: `block_cols`: in each row the entries are distinct and entry 0 is the row's own block within its region; values below 24 name blocks of the row's region, 24 + j the j-th block received from the lower region, 30 + j the j-th from the upper region. `live_blocks`: the first block row of every region has all 12 blocks intact. `halo_lists`: each list holds distinct block indices within the region. bounds[0] < 0 < bounds[1].
All inputs are finite; a program needn't handle non-finite values.
Results may differ from a plain program's by a relative error of at most 0.0005.
The roundings to bfloat16 on the way count: a program that leaves them out, or rounds other values in their place, can miss the bound.
Values may be sent and summed in bfloat16 or wider, within the bound.
A program may use at most 64 MiB of HBM per device.

v0:
```python
import jax
import jax.numpy as jnp
from jax import lax
from jax.sharding import PartitionSpec as P


def shifted(value, axis, steps):
    count = lax.axis_size(axis)
    pairs = [(source, (source + steps) % count) for source in range(count)]
    return lax.ppermute(value, axis, pairs)


def apply_blocks(operand, hessian, block_cols, live_blocks, halo_lists):
    row_blocks = hessian.shape[0]
    block_size = hessian.shape[2]
    mode_count = operand.shape[1]
    shard_blocks = operand.reshape(row_blocks, block_size, mode_count)
    region = lax.all_gather(shard_blocks, "split", axis=0, tiled=True)
    send_lower = region[halo_lists[0, 0]]
    send_upper = region[halo_lists[0, 1]]
    from_lower = shifted(send_upper, "region", 1)
    from_upper = shifted(send_lower, "region", -1)
    candidates = jnp.concatenate([region, from_lower, from_upper], 0)
    picked = candidates[block_cols]
    used_mask = lax.broadcasted_iota(jnp.int32, block_cols.shape, 1) < live_blocks[:, None]
    picked = jnp.where(used_mask[:, :, None, None], picked, jnp.zeros((), jnp.bfloat16))
    product = jnp.einsum("rkij,rkjm->rim", hessian, picked, preferred_element_type=jnp.float32)
    return product.reshape(row_blocks * block_size, mode_count)


def local(vectors, hessian, block_cols, live_blocks, halo_lists, bounds):
    centre = 0.5 * (bounds[0] + bounds[1])
    half_width = 0.5 * (bounds[1] - bounds[0])
    first = apply_blocks(vectors.astype(jnp.bfloat16), hessian, block_cols, live_blocks, halo_lists)
    filtered_one = (first - centre * vectors) / half_width
    second = apply_blocks(
        filtered_one.astype(jnp.bfloat16), hessian, block_cols, live_blocks, halo_lists
    )
    filtered_two = 2.0 * (second - centre * filtered_one) / half_width - vectors
    image = apply_blocks(
        filtered_two.astype(jnp.bfloat16), hessian, block_cols, live_blocks, halo_lists
    )
    total_rows = vectors.shape[0] * lax.axis_size("region") * lax.axis_size("split")
    contract = (((0,), (0,)), ((), ()))
    gram_part = lax.dot_general(
        filtered_two, filtered_two, contract, precision=lax.Precision.HIGHEST
    )
    cross_part = lax.dot_general(filtered_two, image, contract, precision=lax.Precision.HIGHEST)
    gram, cross = lax.psum((gram_part, cross_part), ("region", "split"))
    gram = gram / total_rows
    cross = cross / total_rows
    lower = jnp.linalg.cholesky(gram)
    basis = jax.scipy.linalg.solve_triangular(lower, filtered_two.T, lower=True).T
    partial_left = jax.scipy.linalg.solve_triangular(lower, cross, lower=True)
    projected = jax.scipy.linalg.solve_triangular(lower, partial_left.T, lower=True).T
    return (basis, projected)


def solution(mesh):
    placed = (
        P(("region", "split"), None),
        P(("region", "split"), None, None, None),
        P(("region", "split"), None),
        P(("region", "split")),
        P("region", None, None),
        P(),
    )
    return jax.shard_map(
        local,
        mesh=mesh,
        in_specs=placed,
        out_specs=(P(("region", "split"), None), P()),
        check_vma=False,
    )
```

profile of v0, /device:TPU:1, one launch (start us, length us, event | category | flops | bytes accessed | tf_op | source)
XLA Modules:
  0.0 814.2 jit_solution(8782221556383976657)
XLA Ops:
  10.1 39.6 %all-gather.4.cloned.1.call-done = bf16[24,192,256]{2,1,0:T(8,128)(2,1)} async-done(((bf16[3,192,256]{2,1,0:T(8,128)(2,1)}), bf16[24,192,256]{2,1,0:T(8,128)(2,1)}) %all-gather.4.cloned.1.call-update) | async-done | bytes 2359312 | tf_op jit(solution)/shard_map/all_gather | solution.py:18
  59.0 6.6 collective-permute-start.1
  69.7 4.6 collective-permute-done
  74.3 4.0 collective-permute-done.1
  78.3 3.4 pad_maximum_fusion
  81.7 4.8 gather_fusion.2
  90.6 34.4 %all-gather.6.cloned.1.call-done = bf16[24,192,256]{2,1,0:T(8,128)(2,1)} async-done(((bf16[3,192,256]{2,1,0:T(8,128)(2,1)}), bf16[24,192,256]{2,1,0:T(8,128)(2,1)}) %all-gather.6.cloned.1.call-update) | async-done | bytes 2359312 | tf_op jit(solution)/shard_map/all_gather | solution.py:18
  134.3 6.6 collective-permute-start.3
  141.0 8.7 %collective-permute-done.2 = bf16[6,192,256]{2,1,0:T(8,128)(2,1)} collective-permute-done((bf16[6,192,256]{2,1,0:T(8,128)(2,1)}, bf16[6,192,256]{2,1,0:T(8,128)(2,1)}, u32[]{:S(2)}, u32[]{:S(2)}) %collective-permute-start.2) | collective-permute-done | bytes 589856 | tf_op jit(solution)/shard_map/ppermute | solution.py:10
  149.7 4.0 collective-permute-done.3
  153.7 3.3 pad_maximum_fusion.1
  157.0 4.8 gather_fusion.5
  166.1 34.3 %all-gather.8.cloned.1.call-done = bf16[24,192,256]{2,1,0:T(8,128)(2,1)} async-done(((bf16[3,192,256]{2,1,0:T(8,128)(2,1)}), bf16[24,192,256]{2,1,0:T(8,128)(2,1)}) %all-gather.8.cloned.1.call-update) | async-done | bytes 2359312 | tf_op jit(solution)/shard_map/all_gather | solution.py:18
  209.8 6.6 collective-permute-start.5
  219.6 5.5 collective-permute-done.4
  225.1 4.0 collective-permute-done.5
  229.1 3.3 pad_maximum_fusion.2
  232.5 4.8 gather_fusion.8
  242.3 466.4 %all-reduce.4.cloned.1.call-done = (f32[256,256]{0,1:T(8,128)}, f32[256,256]{0,1:T(8,128)}) async-done(((f32[256,256]{0,1:T(8,128)}, f32[256,256]{0,1:T(8,128)}), (f32[256,256]{0,1:T(8,128)}, f32[256,256]{0,1:T(8,128)})) %all-reduce.4.cloned.1.call-update) | async-done | bytes 524304 | tf_op jit(solution)/shard_map/psum | solution.py:49
  714.8 13.2 %cholesky.50 = f32[128,128]{1,0:T(8,128)} custom-call(f32[128,128]{1,0:T(8,128)} %cholesky.118), custom_call_target="Cholesky" | custom-call | tf_op jit(solution)/shard_map/jit(cholesky)/cholesky | solution.py:52
  731.0 11.3 %custom-call.18 = f32[1,128,128]{1,2,0:T(8,128)} custom-call(f32[1,128,128]{2,1,0:T(8,128)} %get-tuple-element.48), custom_call_target="InvertDiagBlocksLowerTriangular" | custom-call | tf_op jit(solution)/shard_map/jit(cholesky)/cholesky | solution.py:52
  745.7 13.4 %cholesky.105 = f32[128,128]{1,0:T(8,128)} custom-call(f32[128,128]{1,0:T(8,128)} %convolution_subtract_fusion.3), custom_call_target="Cholesky" | custom-call | tf_op jit(solution)/shard_map/jit(cholesky)/cholesky | solution.py:52
  765.0 6.9 while.5
  771.8 21.1 %custom-call.19 = f32[2,128,128]{1,2,0:T(8,128)} custom-call(f32[2,128,128]{2,1,0:T(8,128)} %get-tuple-element.18), custom_call_target="InvertDiagBlocksLowerTriangular" | custom-call | tf_op jit(solution)/shard_map/jit(_solve_triangular)/triangular_solve | solution.py:53
  (85 shorter events, 87.2 us)
Async XLA Ops:
  7.2 79.4 %copy-start = (bf16[3,12,192,192]{3,2,1,0:T(8,128)(2,1)S(1)}, bf16[3,12,192,192]{3,2,1,0:T(8,128)(2,1)}, u32[]{:S(2)}) copy-start(bf16[3,12,192,192]{3,2,1,0:T(8,128)(2,1)} %param.9) | copy-start | bytes 7962628
  7.2 58.4 %copy-start.8 = (f32[2]{0:T(128)S(1)}, f32[2]{0:T(128)}, u32[]{:S(2)}) copy-start(f32[2]{0:T(128)} %param.13) | copy-start | bytes 28
  7.2 61.7 %copy-start.7 = (s32[3,12]{1,0:T(4,128)S(1)}, s32[3,12]{1,0:T(4,128)}, u32[]{:S(2)}) copy-start(s32[3,12]{1,0:T(4,128)} %param.10) | copy-start | bytes 436
  7.2 42.5 %all-gather.4.cloned.1.call-start = ((), (), s32[]{:S(2)}) async-start(), calls=%async_computation | async-start | bytes 2654208 | tf_op jit(solution)/shard_map/all_gather | solution.py:18
  9.2 115.8 %all-gather.6.cloned.1.call-start = ((), (), s32[]{:S(2)}) async-start(), calls=%async_computation.1 | async-start | bytes 2654208 | tf_op jit(solution)/shard_map/all_gather | solution.py:18
  52.8 21.5 %collective-permute-start = (bf16[6,192,256]{2,1,0:T(8,128)(2,1)}, bf16[6,192,256]{2,1,0:T(8,128)(2,1)}, u32[]{:S(2)}, u32[]{:S(2)}) collective-permute-start(bf16[6,192,256]{2,1,0:T(8,128)(2,1)} %gather_fusion), channel_id=1, source_target_pairs={{0,8},{8,16},{16,24},{24,32},{32,40},{40,48},{48,56},{56,64},{64,7... | collective-permute-start | bytes 1769480 | tf_op jit(solution)/shard_map/ppermute | solution.py:10
  59.0 19.3 %collective-permute-start.1 = (bf16[6,192,256]{2,1,0:T(8,128)(2,1)}, bf16[6,192,256]{2,1,0:T(8,128)(2,1)}, u32[]{:S(2)}, u32[]{:S(2)}) collective-permute-start(bf16[6,192,256]{2,1,0:T(8,128)(2,1)} %gather_fusion.1), channel_id=1, source_target_pairs={{0,504},{8,0},{16,8},{24,16},{32,24},{40,32},{48,40},{56,48},{64,5... | collective-permute-start | bytes 1769480 | tf_op jit(solution)/shard_map/ppermute | solution.py:10
  86.6 3.1 copy-start.2
  89.6 0.9 copy-start.4
  90.6 109.9 %all-gather.8.cloned.1.call-start = ((), (), s32[]{:S(2)}) async-start(), calls=%async_computation.2 | async-start | bytes 2654208 | tf_op jit(solution)/shard_map/all_gather | solution.py:18
  128.1 21.5 %collective-permute-start.2 = (bf16[6,192,256]{2,1,0:T(8,128)(2,1)}, bf16[6,192,256]{2,1,0:T(8,128)(2,1)}, u32[]{:S(2)}, u32[]{:S(2)}) collective-permute-start(bf16[6,192,256]{2,1,0:T(8,128)(2,1)} %gather_fusion.3), channel_id=1, source_target_pairs={{0,8},{8,16},{16,24},{24,32},{32,40},{40,48},{48,56},{56,64},{64,7... | collective-permute-start | bytes 1769480 | tf_op jit(solution)/shard_map/ppermute | solution.py:10
  134.3 19.3 %collective-permute-start.3 = (bf16[6,192,256]{2,1,0:T(8,128)(2,1)}, bf16[6,192,256]{2,1,0:T(8,128)(2,1)S(1)}, u32[]{:S(2)}, u32[]{:S(2)}) collective-permute-start(bf16[6,192,256]{2,1,0:T(8,128)(2,1)} %gather_fusion.4), channel_id=1, source_target_pairs={{0,504},{8,0},{16,8},{24,16},{32,24},{40,32},{48,40},{56,48},{64,5... | collective-permute-start | bytes 1769480 | tf_op jit(solution)/shard_map/ppermute | solution.py:10
  161.9 3.1 copy-start.3
  161.9 3.1 copy-start.5
  166.1 542.7 %all-reduce.4.cloned.1.call-start = ((), (), s32[]{:S(2)}) async-start(), calls=%async_computation.3 | async-start | bytes 1048576 | tf_op jit(solution)/shard_map/psum | solution.py:49
  203.6 21.5 %collective-permute-start.4 = (bf16[6,192,256]{2,1,0:T(8,128)(2,1)}, bf16[6,192,256]{2,1,0:T(8,128)(2,1)}, u32[]{:S(2)}, u32[]{:S(2)}) collective-permute-start(bf16[6,192,256]{2,1,0:T(8,128)(2,1)} %gather_fusion.6), channel_id=1, source_target_pairs={{0,8},{8,16},{16,24},{24,32},{32,40},{40,48},{48,56},{56,64},{64,7... | collective-permute-start | bytes 1769480 | tf_op jit(solution)/shard_map/ppermute | solution.py:10
  209.8 19.3 %collective-permute-start.5 = (bf16[6,192,256]{2,1,0:T(8,128)(2,1)}, bf16[6,192,256]{2,1,0:T(8,128)(2,1)S(1)}, u32[]{:S(2)}, u32[]{:S(2)}) collective-permute-start(bf16[6,192,256]{2,1,0:T(8,128)(2,1)} %gather_fusion.7), channel_id=1, source_target_pairs={{0,504},{8,0},{16,8},{24,16},{32,24},{40,32},{48,40},{56,48},{64,5... | collective-permute-start | bytes 1769480 | tf_op jit(solution)/shard_map/ppermute | solution.py:10
  237.3 3.0 copy-start.1
  713.5 0.7 copy-start.6
Sparse Core Ops, SparseCore 0:
  10.7 38.9 all-gather.3
  90.7 34.3 all-gather.5
  166.2 34.2 all-gather.7
  242.4 466.3 all-reduce.3
where the time goes:
time: 816 us; the launch traced here: 814 us
  waiting for transfers between devices  606 us (74%)
  other arithmetic  85.1 us (10%)
  local copies, waits for them, and re-layouts  47.2 us (6%)
  starting transfers between devices  29.3 us (4%)
  matrix products  29 us (4%)
  between operations  18 us (2%)
    psum x1, waiting for transfers between devices, local(): gram, cross = lax.psum((gram_part, cross_part), ('region', 'split'))  466 us
    all_gather x3, waiting for transfers between devices, apply_blocks(): region = lax.all_gather(shard_blocks, 'split', axis=0, tiled=True)  108 us
    another operation x7, other arithmetic, local(): lower = jnp.linalg.cholesky(gram)  42.1 us
    ppermute x6, waiting for transfers between devices, shifted(): return lax.ppermute(value, axis, pairs)  30.8 us
    ppermute x6, starting transfers between devices, shifted(): return lax.ppermute(value, axis, pairs)  29.1 us
    another operation x3, other arithmetic, local(): jax.scipy.linalg.solve_triangular(lower, filtered_two.T, lower=True)  22.8 us
  transfers between devices with their start and end apart: 10, of which 10 were waited for; matrix products, arithmetic and copies ran while one was open for 2% of the time, Pallas kernels for 0%

commit v1 on v0

v1 whole, which is shorter than its diff:
```python
import functools

import jax
import jax.numpy as jnp
from jax import lax
from jax.experimental import pallas as pl
from jax.experimental.pallas import tpu as pltpu
from jax.sharding import PartitionSpec as P

MESH = pl.DeviceIdType.MESH
HIGH = lax.Precision.HIGHEST
X = 4
PIECES = 3
AHEAD = 2
PANEL = 32


def dot_high(a, b, dims=(((1,), (0,)), ((), ()))):
    return lax.dot_general(a, b, dims, precision=HIGH, preferred_element_type=jnp.float32)


def factor_inverse(block):
    size = block.shape[0]
    row_id = lax.broadcasted_iota(jnp.int32, (size, size), 0)
    eye = jnp.where(row_id == lax.broadcasted_iota(jnp.int32, (size, size), 1), 1.0, 0.0)
    work = jnp.concatenate([block, eye.astype(jnp.float32)], axis=1)
    rows = lax.broadcasted_iota(jnp.int32, work.shape, 0)
    for j in range(size):
        scale = lax.rsqrt(work[j : j + 1, j : j + 1])
        row = work[j : j + 1, :] * scale
        column = work[:, j : j + 1] * scale
        work = jnp.where(rows > j, work - column * row, jnp.where(rows == j, row, work))
    return work[:, size:]


def kernel(dims, vec_hbm, hes_hbm, cols, live, lists, bounds, basis, proj, *scratch):
    n_region, n_split, rb, bs, m, nnz, hb, total_rows = dims
    n_z, n_y = n_region // X, n_split // 2
    blocks = rb * n_split
    piece = bs // PIECES
    half_piece = piece // 2
    plane = X * n_split
    chunk = m // plane
    share = hb // 2

    it = iter(scratch)
    vec, hes, hcat, picks = next(it), next(it), next(it), next(it)
    reg = [[next(it) for _ in range(PIECES)] for _ in range(3)]
    hal = [[next(it) for _ in range(PIECES)] for _ in range(3)]
    stg = [[next(it) for _ in range(PIECES)] for _ in range(3)]
    one, two, two_t, img = next(it), next(it), next(it), next(it)
    part = [next(it) for _ in range(2)]
    rs = [next(it) for _ in range(2)]
    zb = [next(it) for _ in range(2)]
    full = [next(it) for _ in range(2)]
    aug = next(it)
    in_sem, g_send, g_recv, h_send, h_recv, a_send, a_recv = (next(it) for _ in range(7))

    r = lax.axis_index("region")
    s = lax.axis_index("split")
    z, x = r // X, r % X
    y, c = s // 2, s % 2
    mate = y * 2 + 1 - c
    up_s = ((y + 1) % n_y) * 2 + c
    down_s = ((y + n_y - 1) % n_y) * 2 + c
    far_s = ((y + 2) % n_y) * 2 + c
    upper = (r + 1) % n_region
    lower = (r + n_region - 1) % n_region
    w = x * n_split + s

    copy_v = pltpu.make_async_copy(vec_hbm, vec, in_sem.at[0])
    copy_h = pltpu.make_async_copy(hes_hbm, hes, in_sem.at[1])
    copy_v.start()
    copy_h.start()

    barrier = pltpu.get_barrier_semaphore()

    def signal(region, split):
        pl.semaphore_signal(barrier, inc=1, device_id=(region, split), device_id_type=MESH)

    def greet_plane(o, carry):
        p = (w + o) % plane
        signal(z * X + p // n_split, p % n_split)
        return carry

    def greet_line(o, carry):
        signal(((z + o) % n_z) * X + x, s)
        return carry

    lax.fori_loop(1, n_z, greet_line, 0)
    lax.fori_loop(1, plane, greet_plane, 0)
    signal(upper, s)
    signal(lower, s)

    def put_own(a, value):
        for q in range(PIECES):
            for b in range(rb):
                reg[a][q][s * rb + b] = value[b * bs + q * piece : b * bs + (q + 1) * piece, :].astype(
                    jnp.bfloat16
                )

    pending = []

    def remote(src, dst, ssem, rsem, region, split):
        copy = pltpu.make_async_remote_copy(
            src_ref=src,
            dst_ref=dst,
            send_sem=ssem,
            recv_sem=rsem,
            device_id=(region, split),
            device_id_type=MESH,
        )
        copy.start()
        pending.append(copy)
        return copy

    def gather_copy(a, q, kind, owner, rows, split):
        view = reg[a][q].at[pl.ds(owner * rb, rb), pl.ds(rows[0], rows[1] - rows[0]), :]
        at = (a * PIECES + q) * 9 + kind
        return remote(view, view, g_send.at[at], g_recv.at[at], r, split)

    whole, low, high = (0, piece), (0, half_piece), (half_piece, piece)

    def wait_gather(a, q, kind, owner, rows):
        view = reg[a][q].at[pl.ds(owner * rb, rb), pl.ds(rows[0], rows[1] - rows[0]), :]
        at = (a * PIECES + q) * 9 + kind
        pltpu.make_async_remote_copy(
            src_ref=view,
            dst_ref=view,
            send_sem=g_send.at[at],
            recv_sem=g_recv.at[at],
            device_id=(r, mate),
            device_id_type=MESH,
        ).wait_recv()

    def send_own(a, q):
        gather_copy(a, q, 0, s, whole, up_s)
        gather_copy(a, q, 1, s, whole, down_s)
        gather_copy(a, q, 4, s, whole, mate)

    def relay(a, q):
        wait_gather(a, q, 0, down_s, whole)
        gather_copy(a, q, 2, down_s, low, up_s)
        wait_gather(a, q, 1, up_s, whole)
        gather_copy(a, q, 3, up_s, high, down_s)
        gather_copy(a, q, 5, down_s, whole, mate)
        gather_copy(a, q, 6, up_s, whole, mate)

    def finish_gather(a, q):
        wait_gather(a, q, 2, far_s, low)
        gather_copy(a, q, 7, far_s, low, mate)
        wait_gather(a, q, 3, far_s, high)
        gather_copy(a, q, 8, far_s, high, mate)
        other = 1 - 2 * c
        wait_gather(a, q, 4, s + other, whole)
        wait_gather(a, q, 5, down_s + other, whole)
        wait_gather(a, q, 6, up_s + other, whole)
        wait_gather(a, q, 7, far_s + other, low)
        wait_gather(a, q, 8, far_s + other, high)

    def halo_view(a, q, d, core):
        return hal[a][q].at[pl.ds((1 - d) * hb + core * share, share)]

    def halo_copy(a, q, d, kind, src, dst, region, split):
        at = ((a * PIECES + q) * 2 + d) * 2 + kind
        return remote(src, dst, h_send.at[at], h_recv.at[at], region, split)

    def wait_halo(a, q, d, kind, core):
        view = halo_view(a, q, d, core)
        at = ((a * PIECES + q) * 2 + d) * 2 + kind
        pltpu.make_async_remote_copy(
            src_ref=view,
            dst_ref=view,
            send_sem=h_send.at[at],
            recv_sem=h_recv.at[at],
            device_id=(r, mate),
            device_id_type=MESH,
        ).wait_recv()

    def send_halo(a, q):
        for d in range(2):
            for j in range(share):
                stg[a][q][d, j] = reg[a][q][lists[0, d, c * share + j]]
            halo_copy(a, q, d, 0, stg[a][q].at[d], halo_view(a, q, d, c), (lower, upper)[d], s)

    def pass_halo(a, q):
        for d in (1, 0):
            wait_halo(a, q, d, 0, c)
            view = halo_view(a, q, d, c)
            halo_copy(a, q, d, 1, view, view, r, mate)

    def finish_halo(a, q):
        for d in (1, 0):
            wait_halo(a, q, d, 1, 1 - c)

    def start_apply(a):
        for q in range(min(AHEAD, PIECES)):
            send_own(a, q)

    def exchange(a, between=None):
        for q in range(PIECES):
            relay(a, q)
            if q + AHEAD < PIECES:
                send_own(a, q + AHEAD)
            if q >= 1:
                finish_gather(a, q - 1)
                send_halo(a, q - 1)
            if q >= 2:
                pass_halo(a, q - 2)
        finish_gather(a, PIECES - 1)
        send_halo(a, PIECES - 1)
        if between is not None:
            between()
        for q in range(max(PIECES - 2, 0), PIECES):
            pass_halo(a, q)
        for q in range(PIECES):
            finish_halo(a, q)

    def multiply(a, i):
        for k in range(nnz):
            col = cols[i, k]
            alive = k < live[i]
            inside = col < blocks
            near = jnp.where(inside, col, 0)
            away = jnp.where(alive, jnp.where(inside, 0, col - blocks), 2 * hb)
            use = jnp.logical_and(alive, inside)
            for q in range(PIECES):
                picks[pl.ds(k * bs + q * piece, piece), :] = jnp.where(
                    use, reg[a][q][near], hal[a][q][away]
                )
        return jnp.dot(hcat[i], picks[...], preferred_element_type=jnp.float32)

    def reduce_send(t):
        def body(o, carry):
            p = (w + o) % plane
            pltpu.make_async_remote_copy(
                src_ref=part[t].at[p],
                dst_ref=rs[t].at[o - 1],
                send_sem=a_send.at[t * 3],
                recv_sem=a_recv.at[t * 3],
                device_id=(z * X + p // n_split, p % n_split),
                device_id_type=MESH,
            ).start()
            return carry

        lax.fori_loop(1, plane, body, 0)

    def bulk(ref, at):
        return pltpu.make_async_remote_copy(
            src_ref=ref,
            dst_ref=ref,
            send_sem=a_send.at[at],
            recv_sem=a_recv.at[at],
            device_id=(r, mate),
            device_id_type=MESH,
        )

    def reduce_line(t):
        bulk(rs[t], t * 3).wait_recv()
        value = part[t][w]
        for o in range(plane - 1):
            value = value + rs[t][o]
        zb[t][z] = value

        def body(o, carry):
            pltpu.make_async_remote_copy(
                src_ref=zb[t].at[z],
                dst_ref=zb[t].at[z],
                send_sem=a_send.at[t * 3 + 1],
                recv_sem=a_recv.at[t * 3 + 1],
                device_id=(((z + o) % n_z) * X + x, s),
                device_id_type=MESH,
            ).start()
            return carry

        lax.fori_loop(1, n_z, body, 0)

    def spread(t):
        bulk(zb[t].at[pl.ds(0, n_z - 1)], t * 3 + 1).wait_recv()
        value = zb[t][0]
        for o in range(1, n_z):
            value = value + zb[t][o]
        full[t][w] = value / total_rows

        def body(o, carry):
            p = (w + o) % plane
            pltpu.make_async_remote_copy(
                src_ref=full[t].at[w],
                dst_ref=full[t].at[w],
                send_sem=a_send.at[t * 3 + 2],
                recv_sem=a_recv.at[t * 3 + 2],
                device_id=(z * X + p // n_split, p % n_split),
                device_id_type=MESH,
            ).start()
            return carry

        lax.fori_loop(1, plane, body, 0)

    def collected(t):
        bulk(full[t].at[pl.ds(0, plane - 1)], t * 3 + 2).wait_recv()
        return full[t][...].reshape(m, m)

    def drain(t):
        bulk(rs[t], t * 3).wait_send()
        bulk(zb[t].at[pl.ds(0, n_z - 1)], t * 3 + 1).wait_send()
        bulk(full[t].at[pl.ds(0, plane - 1)], t * 3 + 2).wait_send()

    for a in range(3):
        for q in range(PIECES):
            hal[a][q][2 * hb] = jnp.zeros((piece, m), jnp.bfloat16)
    copy_v.wait()
    put_own(0, vec[...])
    pl.semaphore_wait(barrier, plane - 1 + n_z - 1 + 2)
    start_apply(0)
    copy_h.wait()

    def join(i, carry):
        for k in range(0, nnz, 2):
            hcat[i, :, k * bs : (k + 2) * bs] = jnp.concatenate([hes[i, k], hes[i, k + 1]], axis=1)
        return carry

    lax.fori_loop(0, rb, join, 0)
    exchange(0)
    centre = 0.5 * (bounds[0] + bounds[1])
    half = 0.5 * (bounds[1] - bounds[0])

    def step_one(i, carry):
        at = pl.ds(pl.multiple_of(i * bs, bs), bs)
        one[at, :] = (multiply(0, i) - centre * vec[at, :]) / half
        return carry

    def step_two(i, carry):
        at = pl.ds(pl.multiple_of(i * bs, bs), bs)
        two[at, :] = 2.0 * (multiply(1, i) - centre * one[at, :]) / half - vec[at, :]
        return carry

    def step_image(i, carry):
        at = pl.ds(pl.multiple_of(i * bs, bs), bs)
        img[at, :] = multiply(2, i)
        return carry

    lax.fori_loop(0, rb, step_one, 0)
    put_own(1, one[...])
    start_apply(1)
    exchange(1)
    lax.fori_loop(0, rb, step_two, 0)
    put_own(2, two[...])
    start_apply(2)
    two_t[...] = two[...].T
    part[0][...] = dot_high(two_t[...], two[...]).reshape(plane, chunk, m)
    reduce_send(0)
    exchange(2, lambda: reduce_line(0))
    lax.fori_loop(0, rb, step_image, 0)
    part[1][...] = dot_high(two_t[...], img[...]).reshape(plane, chunk, m)
    reduce_send(1)
    spread(0)

    row_id = lax.broadcasted_iota(jnp.int32, (m, m), 0)
    col_id = lax.broadcasted_iota(jnp.int32, (m, m), 1)
    aug[:, m:] = jnp.where(row_id == col_id, 1.0, 0.0).astype(jnp.float32)
    aug[:, :m] = collected(0)

    def panel(p):
        at = p * PANEL
        end = at + PANEL
        inverse = factor_inverse(aug[at:end, at:end])
        rows = dot_high(inverse, aug[at:end, :])
        aug[at:end, :] = rows
        if end < m:
            left = rows[:, end:m].T
            aug[end:, :] = aug[end:, :] - dot_high(left, rows)

    panels = m // PANEL
    for p in range(panels // 2):
        panel(p)
    reduce_line(1)
    for p in range(panels // 2, panels):
        panel(p)
    spread(1)
    inverse = aug[:, m:]
    nt = (((1,), (1,)), ((), ()))
    basis[...] = dot_high(two[...], inverse, nt)
    cross = collected(1)
    proj[...] = dot_high(dot_high(inverse, cross), inverse, nt)
    for copy in pending:
        copy.wait_send()
    drain(0)
    drain(1)


def local(sizes, vectors, hessian, block_cols, live_blocks, halo_lists, bounds):
    n_region, n_split = sizes
    rb, nnz, bs, _ = hessian.shape
    m = vectors.shape[1]
    hb = halo_lists.shape[2]
    rows = vectors.shape[0]
    dims = (n_region, n_split, rb, bs, m, nnz, hb, float(rows * n_region * n_split))
    piece = bs // PIECES
    blocks = rb * n_split
    plane = X * n_split
    chunk = m // plane
    n_z = n_region // X
    f32, bf16 = jnp.float32, jnp.bfloat16
    scratch = [
        pltpu.VMEM((rows, m), f32),
        pltpu.VMEM((rb, nnz, bs, bs), bf16),
        pltpu.VMEM((rb, bs, nnz * bs), bf16),
        pltpu.VMEM((nnz * bs, m), bf16),
    ]
    scratch += [pltpu.VMEM((blocks, piece, m), bf16) for _ in range(3 * PIECES)]
    scratch += [pltpu.VMEM((2 * hb + 1, piece, m), bf16) for _ in range(3 * PIECES)]
    scratch += [pltpu.VMEM((2, hb // 2, piece, m), bf16) for _ in range(3 * PIECES)]
    scratch += [
        pltpu.VMEM((rows, m), f32),
        pltpu.VMEM((rows, m), f32),
        pltpu.VMEM((m, rows), f32),
        pltpu.VMEM((rows, m), f32),
    ]
    scratch += [pltpu.VMEM((plane, chunk, m), f32)] * 2
    scratch += [pltpu.VMEM((plane - 1, chunk, m), f32)] * 2
    scratch += [pltpu.VMEM((n_z, chunk, m), f32)] * 2
    scratch += [pltpu.VMEM((plane, chunk, m), f32)] * 2
    scratch += [pltpu.VMEM((m, 2 * m), f32)]
    dma = pltpu.SemaphoreType.DMA
    scratch += [
        dma((2,)),
        dma((27 * PIECES,)),
        dma((27 * PIECES,)),
        dma((12 * PIECES,)),
        dma((12 * PIECES,)),
        dma((6,)),
        dma((6,)),
    ]
    smem = pl.BlockSpec(memory_space=pltpu.SMEM)
    hbm = pl.BlockSpec(memory_space=pl.ANY)
    vmem = pl.BlockSpec(memory_space=pltpu.VMEM)
    return pl.pallas_call(
        functools.partial(kernel, dims),
        out_shape=(jax.ShapeDtypeStruct((rows, m), f32), jax.ShapeDtypeStruct((m, m), f32)),
        in_specs=[hbm, hbm, smem, smem, smem, smem],
        out_specs=(vmem, vmem),
        scratch_shapes=scratch,
        compiler_params=pltpu.CompilerParams(
            collective_id=0, has_side_effects=True, vmem_limit_bytes=58 * 2**20
        ),
    )(vectors, hessian, block_cols, live_blocks, halo_lists, bounds)


def solution(mesh):
    placed = (
        P(("region", "split"), None),
        P(("region", "split"), None, None, None),
        P(("region", "split"), None),
        P(("region", "split")),
        P("region", None, None),
        P(),
    )
    return jax.shard_map(
        functools.partial(local, (mesh.shape["region"], mesh.shape["split"])),
        mesh=mesh,
        in_specs=placed,
        out_specs=(P(("region", "split"), None), P()),
        check_vma=False,
    )
```

time: 816 us -> 150 us (0.18)
  waiting for transfers between devices: 606 us -> 0 us
  Pallas kernels: 0 us -> 145 us
  other arithmetic: 85.1 us -> 0 us
  local copies, waits for them, and re-layouts: 47.2 us -> 3.59 us
  starting transfers between devices: 29.3 us -> 0 us
  matrix products: 29 us -> 0 us
  between operations: 18 us -> 0.64 us
    psum x1 -> x0, waiting for transfers between devices: 466 us -> none  [local(): gram, cross = lax.psum((gram_part, cross_part), ('region', 'split'))]
    pallas_call x0 -> x1, Pallas kernels: none -> 145 us  [local(): pl.pallas_call(functools.partial(kernel, dims), out_shape=(jax.ShapeDtype...]
    all_gather x3 -> x0, waiting for transfers between devices: 108 us -> none  [apply_blocks(): region = lax.all_gather(shard_blocks, 'split', axis=0, tiled=True)]
    another operation x10 -> x0, other arithmetic: 64.9 us -> none  [the longest x7 42.1 us: local(): lower = jnp.linalg.cholesky(gram)]
    gather x9 -> x0, local copies, waits for them, and re-layouts: 33.1 us -> none  [the longest x3 14.5 us: apply_blocks(): picked = candidates[block_cols]]
    ppermute x6 -> x0, waiting for transfers between devices: 30.8 us -> none  [shifted(): return lax.ppermute(value, axis, pairs)]
    ppermute x6 -> x0, starting transfers between devices: 29.1 us -> none  [shifted(): return lax.ppermute(value, axis, pairs)]
    another operation x11 -> x0, matrix products: 14.7 us -> none  [the longest x3 4.02 us: local(): jax.scipy.linalg.solve_triangular(lower, filtered_two.T, lower=True)]
  transfers between devices with their start and end apart: 10 -> 0, of which waited for: 10 -> 0; matrix products, arithmetic and copies ran while one was open for 2% -> 0% of each run, Pallas kernels for 0% -> 0%
where the time goes in v1:
time: 150 us
  Pallas kernels  145 us (97%)
  local copies, waits for them, and re-layouts  3.59 us (2%)
    pallas_call x1, Pallas kernels, local(): pl.pallas_call(functools.partial(kernel, dims), out_shape=(jax.ShapeDtype...  145 us
    unnamed x2, local copies, waits for them, and re-layouts  3.59 us

profile of v1, /device:TPU:1, one launch (start us, length us, event | category | flops | bytes accessed | tf_op | source)
XLA Modules:
  0.0 149.5 jit_solution(1989497048241444869)
XLA Ops:
  0.6 145.3 %shard_map.77 = (f32[576,256]{1,0:T(8,128)}, f32[256,256]{1,0:T(8,128)}) custom-call(f32[576,256]{1,0:T(8,128)} %vec_hbm.1, bf16[3,12,192,192]{3,2,1,0:T(8,128)(2,1)} %hes_hbm.1, s32[3,12]{1,0:T(4,128)} %cols.1, s32[3]{0:T(128)} %live.1, s32[1,2,6]{2,1,0:T(2,128)} %lists.1, f32[2]{0:T(128)} %bounds.1), custom_call_target="tpu_custom_call" | custom-call | tf_op jit(solution)/shard_map/pallas_call | solution.py:437
  145.9 1.9 %copy.10 = f32[576,256]{1,0:T(8,128)} copy(f32[576,256]{1,0:T(8,128)} %get-tuple-element.4) | data formatting | bytes 1179648
  147.8 1.7 %copy.11 = f32[256,256]{1,0:T(8,128)} copy(f32[256,256]{1,0:T(8,128)} %get-tuple-element.5) | data formatting | bytes 524288

commit v2 on v1

--- a/solution.py
+++ b/solution.py
@@ -12,7 +12,10 @@
 X = 4
 PIECES = 3
 AHEAD = 2
-PANEL = 32
+PANEL = 64
+GROUP = 16
+RS_AT, LINE_AT = ("relay", 2), ("pass", 0)
+SPREAD_AT = 3
 
 
 def dot_high(a, b, dims=(((1,), (0,)), ((), ()))):
@@ -22,15 +25,22 @@
 def factor_inverse(block):
     size = block.shape[0]
     row_id = lax.broadcasted_iota(jnp.int32, (size, size), 0)
-    eye = jnp.where(row_id == lax.broadcasted_iota(jnp.int32, (size, size), 1), 1.0, 0.0)
-    work = jnp.concatenate([block, eye.astype(jnp.float32)], axis=1)
+    same = row_id == lax.broadcasted_iota(jnp.int32, (size, size), 1)
+    work = jnp.concatenate([block, jnp.where(same, 1.0, 0.0).astype(jnp.float32)], axis=1)
     rows = lax.broadcasted_iota(jnp.int32, work.shape, 0)
-    for j in range(size):
-        scale = lax.rsqrt(work[j : j + 1, j : j + 1])
-        row = work[j : j + 1, :] * scale
-        column = work[:, j : j + 1] * scale
-        work = jnp.where(rows > j, work - column * row, jnp.where(rows == j, row, work))
-    return work[:, size:]
+    for first in range(0, size, GROUP):
+        wide = [
+            jnp.broadcast_to(work[:, first + t : first + t + 1], work.shape) for t in range(GROUP)
+        ]
+        for t in range(GROUP):
+            j = first + t
+            over = 1.0 / wide[t][j : j + 1, :]
+            below = jnp.where(rows > j, wide[t], 0.0)
+            work = work - below * (work[j : j + 1, :] * over)
+            for u in range(t + 1, GROUP):
+                wide[u] = wide[u] - below * (wide[u][j : j + 1, :] * over)
+    pivots = jnp.sum(jnp.where(same, work[:, :size], 0.0), axis=1, keepdims=True)
+    return work[:, size:] * lax.rsqrt(pivots)
 
 
 def kernel(dims, vec_hbm, hes_hbm, cols, live, lists, bounds, basis, proj, *scratch):
@@ -54,7 +64,7 @@
     zb = [next(it) for _ in range(2)]
     full = [next(it) for _ in range(2)]
     aug = next(it)
-    in_sem, g_send, g_recv, h_send, h_recv, a_send, a_recv = (next(it) for _ in range(7))
+    in_sem, g_send, g_recv, h_send, h_recv, a_send, a_recv, token = (next(it) for _ in range(8))
 
     r = lax.axis_index("region")
     s = lax.axis_index("split")
@@ -78,19 +88,49 @@
     def signal(region, split):
         pl.semaphore_signal(barrier, inc=1, device_id=(region, split), device_id_type=MESH)
 
-    def greet_plane(o, carry):
-        p = (w + o) % plane
-        signal(z * X + p // n_split, p % n_split)
+    def greet_split(o, carry):
+        signal(r, (s + o) % n_split)
         return carry
 
-    def greet_line(o, carry):
-        signal(((z + o) % n_z) * X + x, s)
-        return carry
-
-    lax.fori_loop(1, n_z, greet_line, 0)
-    lax.fori_loop(1, plane, greet_plane, 0)
-    signal(upper, s)
-    signal(lower, s)
+    ring = (
+        (z * X + (x + 1) % X, z * X + (x + X - 1) % X),
+        (((z + 1) % n_z) * X + x, ((z + n_z - 1) % n_z) * X + x),
+    )
+    for region in (upper, lower) + ring[1] + ring[0]:
+        signal(region, s)
+    lax.fori_loop(1, n_split, greet_split, 0)
+
+    rounds = (X // 2, max(n_z // 2 - 1, 0))
+    ticks = []
+
+    def pass_tokens(k):
+        for axis in range(2):
+            for side in range(2):
+                if k <= rounds[axis]:
+                    if k > 1:
+                        pl.semaphore_wait(token.at[axis, k - 2, side], 1)
+        for axis in range(2):
+            for side in range(2):
+                if k <= rounds[axis]:
+                    pl.semaphore_signal(
+                        token.at[axis, k - 1, side],
+                        inc=1,
+                        device_id=(ring[axis][side], s),
+                        device_id_type=MESH,
+                    )
+
+    def tick():
+        if len(ticks) < max(rounds):
+            ticks.append(0)
+            pass_tokens(len(ticks))
+
+    def all_ticks():
+        while len(ticks) < max(rounds):
+            tick()
+        for axis in range(2):
+            for side in range(2):
+                if rounds[axis] > 0:
+                    pl.semaphore_wait(token.at[axis, rounds[axis] - 1, side], 1)
 
     def put_own(a, value):
         for q in range(PIECES):
@@ -197,22 +237,30 @@
         for q in range(min(AHEAD, PIECES)):
             send_own(a, q)
 
-    def exchange(a, between=None):
+    def exchange(a, hooks=()):
+        hooks = dict(hooks)
+
+        def reached(name, q):
+            if (name, q) in hooks:
+                hooks[name, q]()
+
         for q in range(PIECES):
             relay(a, q)
             if q + AHEAD < PIECES:
                 send_own(a, q + AHEAD)
+            tick()
+            reached("relay", q)
             if q >= 1:
                 finish_gather(a, q - 1)
                 send_halo(a, q - 1)
-            if q >= 2:
-                pass_halo(a, q - 2)
+                reached("select", q - 1)
         finish_gather(a, PIECES - 1)
         send_halo(a, PIECES - 1)
-        if between is not None:
-            between()
-        for q in range(max(PIECES - 2, 0), PIECES):
+        reached("select", PIECES - 1)
+        tick()
+        for q in range(PIECES):
             pass_halo(a, q)
+            reached("pass", q)
         for q in range(PIECES):
             finish_halo(a, q)
 
@@ -243,7 +291,8 @@
             ).start()
             return carry
 
-        lax.fori_loop(1, plane, body, 0)
+        lax.fori_loop(plane // 2, plane, body, 0)
+        lax.fori_loop(1, plane // 2, body, 0)
 
     def bulk(ref, at):
         return pltpu.make_async_remote_copy(
@@ -268,12 +317,12 @@
                 dst_ref=zb[t].at[z],
                 send_sem=a_send.at[t * 3 + 1],
                 recv_sem=a_recv.at[t * 3 + 1],
-                device_id=(((z + o) % n_z) * X + x, s),
+                device_id=(((z + n_z // 2 + (1 - 2 * (o % 2)) * ((o + 1) // 2)) % n_z) * X + x, s),
                 device_id_type=MESH,
             ).start()
             return carry
 
-        lax.fori_loop(1, n_z, body, 0)
+        lax.fori_loop(0, n_z - 1, body, 0)
 
     def spread(t):
         bulk(zb[t].at[pl.ds(0, n_z - 1)], t * 3 + 1).wait_recv()
@@ -294,7 +343,8 @@
             ).start()
             return carry
 
-        lax.fori_loop(1, plane, body, 0)
+        lax.fori_loop(plane // 2, plane, body, 0)
+        lax.fori_loop(1, plane // 2, body, 0)
 
     def collected(t):
         bulk(full[t].at[pl.ds(0, plane - 1)], t * 3 + 2).wait_recv()
@@ -310,7 +360,7 @@
             hal[a][q][2 * hb] = jnp.zeros((piece, m), jnp.bfloat16)
     copy_v.wait()
     put_own(0, vec[...])
-    pl.semaphore_wait(barrier, plane - 1 + n_z - 1 + 2)
+    pl.semaphore_wait(barrier, n_split - 1 + 6)
     start_apply(0)
     copy_h.wait()
 
@@ -348,12 +398,19 @@
     start_apply(2)
     two_t[...] = two[...].T
     part[0][...] = dot_high(two_t[...], two[...]).reshape(plane, chunk, m)
-    reduce_send(0)
-    exchange(2, lambda: reduce_line(0))
+    all_ticks()
+    exchange(
+        2,
+        {
+            RS_AT: lambda: reduce_send(0),
+            LINE_AT: lambda: reduce_line(0),
+        },
+    )
     lax.fori_loop(0, rb, step_image, 0)
     part[1][...] = dot_high(two_t[...], img[...]).reshape(plane, chunk, m)
     reduce_send(1)
     spread(0)
+    reduce_line(1)
 
     row_id = lax.broadcasted_iota(jnp.int32, (m, m), 0)
     col_id = lax.broadcasted_iota(jnp.int32, (m, m), 1)
@@ -371,12 +428,10 @@
             aug[end:, :] = aug[end:, :] - dot_high(left, rows)
 
     panels = m // PANEL
-    for p in range(panels // 2):
+    for p in range(panels):
         panel(p)
-    reduce_line(1)
-    for p in range(panels // 2, panels):
-        panel(p)
-    spread(1)
+        if p == SPREAD_AT:
+            spread(1)
     inverse = aug[:, m:]
     nt = (((1,), (1,)), ((), ()))
     basis[...] = dot_high(two[...], inverse, nt)
@@ -430,6 +485,7 @@
         dma((12 * PIECES,)),
         dma((6,)),
         dma((6,)),
+        pltpu.SemaphoreType.REGULAR((2, 8, 2)),
     ]
     smem = pl.BlockSpec(memory_space=pltpu.SMEM)
     hbm = pl.BlockSpec(memory_space=pl.ANY)

time: 150 us -> 121 us (0.81)
  Pallas kernels: 145 us -> 116 us
    pallas_call x1, Pallas kernels: 145 us -> 116 us  [local(): pl.pallas_call(functools.partial(kernel, dims), out_shape=(jax.ShapeDtype...]
where the time goes in v2:
time: 121 us; the launch traced here: 120 us
  Pallas kernels  116 us (96%)
  local copies, waits for them, and re-layouts  3.59 us (3%)
    pallas_call x1, Pallas kernels, local(): pl.pallas_call(functools.partial(kernel, dims), out_shape=(jax.ShapeDtype...  116 us
    unnamed x2, local copies, waits for them, and re-layouts  3.59 us

profile of v2, /device:TPU:1, one launch (start us, length us, event | category | flops | bytes accessed | tf_op | source)
XLA Modules:
  0.0 120.3 jit_solution(13198052138864789872)
XLA Ops:
  0.6 116.1 %shard_map.77 = (f32[576,256]{1,0:T(8,128)}, f32[256,256]{1,0:T(8,128)}) custom-call(f32[576,256]{1,0:T(8,128)} %vec_hbm.1, bf16[3,12,192,192]{3,2,1,0:T(8,128)(2,1)} %hes_hbm.1, s32[3,12]{1,0:T(4,128)} %cols.1, s32[3]{0:T(128)} %live.1, s32[1,2,6]{2,1,0:T(2,128)} %lists.1, f32[2]{0:T(128)} %bounds.1), custom_call_target="tpu_custom_call" | custom-call | tf_op jit(solution)/shard_map/pallas_call | solution.py:493
  116.7 1.9 %copy.10 = f32[576,256]{1,0:T(8,128)} copy(f32[576,256]{1,0:T(8,128)} %get-tuple-element.4) | data formatting | bytes 1179648
  118.6 1.7 %copy.11 = f32[256,256]{1,0:T(8,128)} copy(f32[256,256]{1,0:T(8,128)} %get-tuple-element.5) | data formatting | bytes 524288

commit v3 on v2

--- a/solution.py
+++ b/solution.py
@@ -9,13 +9,14 @@
 
 MESH = pl.DeviceIdType.MESH
 HIGH = lax.Precision.HIGHEST
+TRANSPOSED = (((1,), (1,)), ((), ()))
 X = 4
 PIECES = 3
 AHEAD = 2
 PANEL = 64
 GROUP = 16
-RS_AT, LINE_AT = ("relay", 2), ("pass", 0)
-SPREAD_AT = 3
+RS_AT, LINE_AT = ("select", 0), ("pass", 0)
+SPREAD_AT = 2
 
 
 def dot_high(a, b, dims=(((1,), (0,)), ((), ()))):
@@ -43,7 +44,7 @@
     return work[:, size:] * lax.rsqrt(pivots)
 
 
-def kernel(dims, vec_hbm, hes_hbm, cols, live, lists, bounds, basis, proj, *scratch):
+def kernel(dims, vec_hbm, hes_hbm, cols, live, lists, bounds, basis, inv_out, cross_out, *scratch):
     n_region, n_split, rb, bs, m, nnz, hb, total_rows = dims
     n_z, n_y = n_region // X, n_split // 2
     blocks = rb * n_split
@@ -62,9 +63,12 @@
     part = [next(it) for _ in range(2)]
     rs = [next(it) for _ in range(2)]
     zb = [next(it) for _ in range(2)]
-    full = [next(it) for _ in range(2)]
+    gram_full, own_chunk = next(it), [next(it) for _ in range(2)]
+    full = [gram_full, cross_out]
     aug = next(it)
-    in_sem, g_send, g_recv, h_send, h_recv, a_send, a_recv, token = (next(it) for _ in range(8))
+    in_sem, g_send, g_recv, h_send, h_recv, a_send, a_recv, token, out_sem = (
+        next(it) for _ in range(9)
+    )
 
     r = lax.axis_index("region")
     s = lax.axis_index("split")
@@ -248,7 +252,8 @@
             relay(a, q)
             if q + AHEAD < PIECES:
                 send_own(a, q + AHEAD)
-            tick()
+            if a == 1:
+                tick()
             reached("relay", q)
             if q >= 1:
                 finish_gather(a, q - 1)
@@ -260,6 +265,8 @@
         tick()
         for q in range(PIECES):
             pass_halo(a, q)
+            if a == 0:
+                tick()
             reached("pass", q)
         for q in range(PIECES):
             finish_halo(a, q)
@@ -329,12 +336,13 @@
         value = zb[t][0]
         for o in range(1, n_z):
             value = value + zb[t][o]
-        full[t][w] = value / total_rows
+        own_chunk[t][...] = value / total_rows
+        pltpu.make_async_copy(own_chunk[t], full[t].at[w], out_sem.at[t]).start()
 
         def body(o, carry):
             p = (w + o) % plane
             pltpu.make_async_remote_copy(
-                src_ref=full[t].at[w],
+                src_ref=own_chunk[t],
                 dst_ref=full[t].at[w],
                 send_sem=a_send.at[t * 3 + 2],
                 recv_sem=a_recv.at[t * 3 + 2],
@@ -348,7 +356,7 @@
 
     def collected(t):
         bulk(full[t].at[pl.ds(0, plane - 1)], t * 3 + 2).wait_recv()
-        return full[t][...].reshape(m, m)
+        pltpu.make_async_copy(own_chunk[t], full[t].at[w], out_sem.at[t]).wait()
 
     def drain(t):
         bulk(rs[t], t * 3).wait_send()
@@ -415,7 +423,8 @@
     row_id = lax.broadcasted_iota(jnp.int32, (m, m), 0)
     col_id = lax.broadcasted_iota(jnp.int32, (m, m), 1)
     aug[:, m:] = jnp.where(row_id == col_id, 1.0, 0.0).astype(jnp.float32)
-    aug[:, :m] = collected(0)
+    collected(0)
+    aug[:, :m] = gram_full[...].reshape(m, m)
 
     def panel(p):
         at = p * PANEL
@@ -432,15 +441,37 @@
         panel(p)
         if p == SPREAD_AT:
             spread(1)
-    inverse = aug[:, m:]
-    nt = (((1,), (1,)), ((), ()))
-    basis[...] = dot_high(two[...], inverse, nt)
-    cross = collected(1)
-    proj[...] = dot_high(dot_high(inverse, cross), inverse, nt)
+    copy_inv = pltpu.make_async_copy(aug.at[:, pl.ds(m, m)], inv_out, out_sem.at[2])
+    copy_inv.start()
+    one[...] = dot_high(two[...], aug[:, m:], TRANSPOSED)
+    copy_basis = pltpu.make_async_copy(one, basis, out_sem.at[3])
+    copy_basis.start()
     for copy in pending:
         copy.wait_send()
     drain(0)
     drain(1)
+    copy_inv.wait()
+    copy_basis.wait()
+    collected(1)
+
+
+def finish(basis_in, inv_in, cross_in, basis_out, proj_out, basis, inv, cross, proj, sem):
+    inputs = [
+        pltpu.make_async_copy(a, b, sem.at[i])
+        for i, (a, b) in enumerate(((inv_in, inv), (cross_in, cross), (basis_in, basis)))
+    ]
+    for copy in inputs:
+        copy.start()
+    inputs[0].wait()
+    inputs[1].wait()
+    proj[...] = dot_high(dot_high(inv[...], cross[...]), inv[...], TRANSPOSED)
+    copy_proj = pltpu.make_async_copy(proj, proj_out, sem.at[3])
+    copy_proj.start()
+    inputs[2].wait()
+    copy_basis = pltpu.make_async_copy(basis, basis_out, sem.at[4])
+    copy_basis.start()
+    copy_proj.wait()
+    copy_basis.wait()
 
 
 def local(sizes, vectors, hessian, block_cols, live_blocks, halo_lists, bounds):
@@ -474,7 +505,8 @@
     scratch += [pltpu.VMEM((plane, chunk, m), f32)] * 2
     scratch += [pltpu.VMEM((plane - 1, chunk, m), f32)] * 2
     scratch += [pltpu.VMEM((n_z, chunk, m), f32)] * 2
-    scratch += [pltpu.VMEM((plane, chunk, m), f32)] * 2
+    scratch += [pltpu.VMEM((plane, chunk, m), f32)]
+    scratch += [pltpu.VMEM((chunk, m), f32)] * 2
     scratch += [pltpu.VMEM((m, 2 * m), f32)]
     dma = pltpu.SemaphoreType.DMA
     scratch += [
@@ -486,20 +518,38 @@
         dma((6,)),
         dma((6,)),
         pltpu.SemaphoreType.REGULAR((2, 8, 2)),
+        dma((4,)),
     ]
     smem = pl.BlockSpec(memory_space=pltpu.SMEM)
     hbm = pl.BlockSpec(memory_space=pl.ANY)
-    vmem = pl.BlockSpec(memory_space=pltpu.VMEM)
-    return pl.pallas_call(
+    basis, inverse, cross = pl.pallas_call(
         functools.partial(kernel, dims),
-        out_shape=(jax.ShapeDtypeStruct((rows, m), f32), jax.ShapeDtypeStruct((m, m), f32)),
+        out_shape=(
+            jax.ShapeDtypeStruct((rows, m), f32),
+            jax.ShapeDtypeStruct((m, m), f32),
+            jax.ShapeDtypeStruct((plane, chunk, m), f32),
+        ),
         in_specs=[hbm, hbm, smem, smem, smem, smem],
-        out_specs=(vmem, vmem),
+        out_specs=(hbm, hbm, hbm),
         scratch_shapes=scratch,
         compiler_params=pltpu.CompilerParams(
             collective_id=0, has_side_effects=True, vmem_limit_bytes=58 * 2**20
         ),
     )(vectors, hessian, block_cols, live_blocks, halo_lists, bounds)
+    return pl.pallas_call(
+        finish,
+        out_shape=(jax.ShapeDtypeStruct((rows, m), f32), jax.ShapeDtypeStruct((m, m), f32)),
+        in_specs=[hbm, hbm, hbm],
+        out_specs=(hbm, hbm),
+        scratch_shapes=[
+            pltpu.VMEM((rows, m), f32),
+            pltpu.VMEM((m, m), f32),
+            pltpu.VMEM((m, m), f32),
+            pltpu.VMEM((m, m), f32),
+            dma((5,)),
+        ],
+        compiler_params=pltpu.CompilerParams(vmem_limit_bytes=58 * 2**20),
+    )(basis, inverse, cross.reshape(m, m))
 
 
 def solution(mesh):

time: 121 us -> 116 us (0.959)
  local copies, waits for them, and re-layouts: 3.59 us -> 0 us
    unnamed x2 -> x0, local copies, waits for them, and re-layouts: 3.59 us -> none
    pallas_call x1, Pallas kernels: 116 us -> 113 us  [local(): pl.pallas_call(functools.partial(kernel, dims), out_shape=(jax.ShapeDtype...]
    pallas_call x0 -> x1, Pallas kernels: none -> 2.98 us  [local(): pl.pallas_call(finish, out_shape=(jax.ShapeDtypeStruct((rows, m), f32), j...]
where the time goes in v3:
time: 116 us
  Pallas kernels  116 us (100%)
    pallas_call x1, Pallas kernels, local(): pl.pallas_call(functools.partial(kernel, dims), out_shape=(jax.ShapeDtype...  113 us
    pallas_call x1, Pallas kernels, local(): pl.pallas_call(finish, out_shape=(jax.ShapeDtypeStruct((rows, m), f32), j...  2.98 us

profile of v3, /device:TPU:1, one launch (start us, length us, event | category | flops | bytes accessed | tf_op | source)
XLA Modules:
  0.0 116.3 jit_solution(5623787884993349113)
XLA Ops:
  0.6 112.5 %shard_map.77 = (f32[576,256]{1,0:T(8,128)}, f32[256,256]{1,0:T(8,128)}, f32[32,8,256]{2,1,0:T(8,128)}) custom-call(f32[576,256]{1,0:T(8,128)} %vec_hbm.1, bf16[3,12,192,192]{3,2,1,0:T(8,128)(2,1)} %hes_hbm.1, s32[3,12]{1,0:T(4,128)} %cols.1, s32[3]{0:T(128)} %live.1, s32[1,2,6]{2,1,0:T(2,128)} %lists.1, f32[2]{0:T(128)} %bounds.1), custom_call_target="tpu_custom_call" | custom-call | tf_op jit(solution)/shard_map/pallas_call | solution.py:525
  113.2 3.0 %shard_map.78 = (f32[576,256]{1,0:T(8,128)}, f32[256,256]{1,0:T(8,128)}) custom-call(f32[576,256]{1,0:T(8,128)} %get-tuple-element.5.basis_in, f32[256,256]{1,0:T(8,128)} %get-tuple-element.6.inv_in, f32[256,256]{1,0:T(8,128)} %bitcast.1), custom_call_target="tpu_custom_call" | custom-call | tf_op jit(solution)/shard_map/pallas_call | solution.py:539

commit v4 on v3

--- a/solution.py
+++ b/solution.py
@@ -44,7 +44,8 @@
     return work[:, size:] * lax.rsqrt(pivots)
 
 
-def kernel(dims, vec_hbm, hes_hbm, cols, live, lists, bounds, basis, inv_out, cross_out, *scratch):
+def kernel(dims, vec_hbm, hes_hbm, *refs):
+    tables_hbm, (basis, inv_out, cross_out), scratch = refs[:4], refs[4:7], refs[7:]
     n_region, n_split, rb, bs, m, nnz, hb, total_rows = dims
     n_z, n_y = n_region // X, n_split // 2
     blocks = rb * n_split
@@ -55,6 +56,8 @@
     share = hb // 2
 
     it = iter(scratch)
+    tables = [next(it) for _ in range(4)]
+    cols, live, lists, bounds = tables
     vec, hes, hcat, picks = next(it), next(it), next(it), next(it)
     reg = [[next(it) for _ in range(PIECES)] for _ in range(3)]
     hal = [[next(it) for _ in range(PIECES)] for _ in range(3)]
@@ -85,6 +88,12 @@
     copy_v = pltpu.make_async_copy(vec_hbm, vec, in_sem.at[0])
     copy_h = pltpu.make_async_copy(hes_hbm, hes, in_sem.at[1])
     copy_v.start()
+    copies = [
+        pltpu.make_async_copy(a, b, in_sem.at[2 + i])
+        for i, (a, b) in enumerate(zip(tables_hbm, tables))
+    ]
+    for copy in copies:
+        copy.start()
     copy_h.start()
 
     barrier = pltpu.get_barrier_semaphore()
@@ -370,6 +379,8 @@
     put_own(0, vec[...])
     pl.semaphore_wait(barrier, n_split - 1 + 6)
     start_apply(0)
+    for copy in copies:
+        copy.wait()
     copy_h.wait()
 
     def join(i, carry):
@@ -487,7 +498,8 @@
     chunk = m // plane
     n_z = n_region // X
     f32, bf16 = jnp.float32, jnp.bfloat16
-    scratch = [
+    scratch = [pltpu.SMEM(a.shape, a.dtype) for a in (block_cols, live_blocks, halo_lists, bounds)]
+    scratch += [
         pltpu.VMEM((rows, m), f32),
         pltpu.VMEM((rb, nnz, bs, bs), bf16),
         pltpu.VMEM((rb, bs, nnz * bs), bf16),
@@ -510,7 +522,7 @@
     scratch += [pltpu.VMEM((m, 2 * m), f32)]
     dma = pltpu.SemaphoreType.DMA
     scratch += [
-        dma((2,)),
+        dma((6,)),
         dma((27 * PIECES,)),
         dma((27 * PIECES,)),
         dma((12 * PIECES,)),
@@ -520,7 +532,6 @@
         pltpu.SemaphoreType.REGULAR((2, 8, 2)),
         dma((4,)),
     ]
-    smem = pl.BlockSpec(memory_space=pltpu.SMEM)
     hbm = pl.BlockSpec(memory_space=pl.ANY)
     basis, inverse, cross = pl.pallas_call(
         functools.partial(kernel, dims),
@@ -529,7 +540,7 @@
             jax.ShapeDtypeStruct((m, m), f32),
             jax.ShapeDtypeStruct((plane, chunk, m), f32),
         ),
-        in_specs=[hbm, hbm, smem, smem, smem, smem],
+        in_specs=[hbm] * 6,
         out_specs=(hbm, hbm, hbm),
         scratch_shapes=scratch,
         compiler_params=pltpu.CompilerParams(

time: 116 us -> 116 us (level)
  no operation moved by 1% of the time
where the time goes in v4:
time: 116 us
  Pallas kernels  115 us (99%)
    pallas_call x1, Pallas kernels, local(): pl.pallas_call(functools.partial(kernel, dims), out_shape=(jax.ShapeDtype...  112 us
    pallas_call x1, Pallas kernels, local(): pl.pallas_call(finish, out_shape=(jax.ShapeDtypeStruct((rows, m), f32), j...  2.98 us

profile of v4, /device:TPU:1, one launch (start us, length us, event | category | flops | bytes accessed | tf_op | source)
XLA Modules:
  0.0 115.5 jit_solution(8891344869505082944)
XLA Ops:
  0.6 111.7 %shard_map.77 = (f32[576,256]{1,0:T(8,128)}, f32[256,256]{1,0:T(8,128)}, f32[32,8,256]{2,1,0:T(8,128)}) custom-call(f32[576,256]{1,0:T(8,128)} %vec_hbm.1, bf16[3,12,192,192]{3,2,1,0:T(8,128)(2,1)} %hes_hbm.1, s32[3,12]{1,0:T(4,128)} %refs_0_.1, s32[3]{0:T(128)} %refs_1_.1, s32[1,2,6]{2,1,0:T(2,128)} %refs_2_.1, f32[2]{0:T(128)} %refs_3_.1), custom_call_target="tpu_custom_call" | custom-call | tf_op jit(solution)/shard_map/pallas_call | solution.py:536
  112.4 3.0 %shard_map.78 = (f32[576,256]{1,0:T(8,128)}, f32[256,256]{1,0:T(8,128)}) custom-call(f32[576,256]{1,0:T(8,128)} %get-tuple-element.5.basis_in, f32[256,256]{1,0:T(8,128)} %get-tuple-element.6.inv_in, f32[256,256]{1,0:T(8,128)} %bitcast.1), custom_call_target="tpu_custom_call" | custom-call | tf_op jit(solution)/shard_map/pallas_call | solution.py:550
